TPU v7x, 256 devices: a whole 4x4x8 slice. The times are simulated.
256 devices in a mesh: date: 64 (over z, x, core), pix: 4 (over y).
Axes of the slice: x: 4, y: 4, z: 8, core: 2. Of those that a mesh axis runs over, the one named last changes fastest.
Arguments:
- stack: bfloat16 [64, 10, 32, 2048], P('date', None, 'pix'), may hold values from -4 to 12
- cloud: int32 [64, 32, 2048], P('date', 'pix'), may hold values 0 or 1
Outputs:
- composite: float32 [10, 32, 2048], P(None, 'pix')
All inputs are finite; a program needn't handle non-finite values. No bound on the sum of `cloud` on one device may be relied on, other than what follows from the above.
Results may differ from a plain program's by a relative error of at most 0.0003.
Values may be sent and summed in bfloat16 or wider, within the bound.
A program may use at most 64 MiB of HBM per device.

v0:
```python
import jax
import jax.numpy as jnp
from jax import lax
from jax.sharding import Mesh
from jax.sharding import PartitionSpec as P

ITERS = 2
DATE = ("date_0", "date_1", "date_2")


delta_sq = 0.01
eps = 1e-05


def with_halo(cells, sides, width):
    for axis, dim in sides:
        count = lax.axis_size(axis)
        ends = count - 1
        head = lax.slice_in_dim(cells, 0, width, axis=dim)
        tail = lax.slice_in_dim(cells, cells.shape[dim] - width, cells.shape[dim], axis=dim)
        cells = jnp.concatenate(
            [
                lax.ppermute(tail, axis, [(i, (i + 1) % count) for i in range(ends)]),
                cells,
                lax.ppermute(head, axis, [((i + 1) % count, i) for i in range(ends)]),
            ],
            axis=dim,
        )
    return cells


def padded_to(lines, count):
    spare = -lines.shape[0] % count
    if not spare:
        return lines
    return jnp.concatenate([lines, jnp.zeros((spare, *lines.shape[1:]), lines.dtype)])


def from_everyone(shard, axis):
    count = lax.axis_size(axis)
    return lax.all_to_all(
        jnp.broadcast_to(shard[None], (count, *shard.shape)), axis, 0, 0, tiled=True
    )


def laid_out(parts, dim):
    parts = jnp.moveaxis(parts, 0, dim)
    lengths = parts.shape
    return parts.reshape(*lengths[:dim], lengths[dim] * lengths[dim + 1], *lengths[dim + 2 :])


def gathered_by_axis(shard, axes, dim):
    far, near = axes
    first = from_everyone(shard, far)
    parts = jnp.swapaxes(from_everyone(first, near), 0, 1)
    return laid_out(parts.reshape(-1, *shard.shape), dim)


def in_blocks(shard, dim, count):
    before, after = (shard.shape[:dim], shard.shape[dim + 1 :])
    return jnp.moveaxis(shard.reshape(*before, count, -1, *after), dim, 0)


def sum_at_owner(shard, axis, dim):
    parts = in_blocks(shard, dim, lax.axis_size(axis))
    arrived = lax.all_to_all(parts, axis, split_axis=0, concat_axis=0, tiled=True)
    return arrived.sum(axis=0)


def summed_rows(shard, axes, dim):
    far, near = axes
    own = sum_at_owner(in_blocks(shard, dim, lax.axis_size(far)), near, dim + 1)
    return jnp.sum(lax.all_to_all(own, far, 0, 0, tiled=True), axis=0)


def total_of(shard, axes):
    padded = padded_to(shard, lax.axis_size(axes[0]) * lax.axis_size(axes[1]))
    whole = gathered_by_axis(summed_rows(padded, axes, 0), axes, 0)
    return lax.slice_in_dim(whole, 0, len(shard)).reshape(shard.shape)


def in_one(arrays, axis):
    ends = [0]
    for a in arrays:
        ends.append(ends[-1] + a.size)
    total = total_of(jnp.concatenate([a.ravel() for a in arrays]), axis)
    return tuple((total[b:e].reshape(a.shape) for a, b, e in zip(arrays, ends, ends[1:])))


def over_copies(shard, axis):
    return from_everyone(shard, axis).sum(axis=0)


def packed_total(arrays, axis):
    ends = [0]
    for a in arrays:
        ends.append(ends[-1] + a.size)
    total = over_copies(jnp.concatenate([a.ravel() for a in arrays]), axis)
    return tuple((total[b:e].reshape(a.shape) for a, b, e in zip(arrays, ends, ends[1:])))


def local_sums(values, valid, median, first):
    if first:
        weight = valid
    else:
        diff = values - median[None]
        weight = valid / jnp.sqrt(jnp.sum(diff * diff, axis=1) + delta_sq)
    numer = jnp.sum(weight[:, None] * values, axis=0)
    denom = jnp.sum(weight, axis=0, keepdims=True)
    return (numer, denom)


def moments(median):
    return (jnp.sum(median, axis=(1, 2)), jnp.sum(median * median, axis=(1, 2)))


def standardize(median, first_sum, second_sum, count):
    mean = first_sum / count
    var = second_sum / count - mean * mean
    return (median - mean[:, None, None]) / jnp.sqrt(var[:, None, None] + eps)


def body(stack, cloud):
    bands = stack.shape[1]
    rows = stack.shape[2]
    cols = stack.shape[3]
    cloudy = (1 - cloud).astype(jnp.bfloat16)
    rimmed = with_halo(cloudy, (("pix", 1),), 1).astype(jnp.float32)
    padded = jnp.pad(rimmed, ((0, 0), (0, 0), (1, 1)))
    near = jnp.maximum(padded[:, 1:-1, 1:-1], padded[:, 2:, 1:-1])
    near = jnp.maximum(near, padded[:, :-2, 1:-1])
    near = jnp.maximum(near, padded[:, 1:-1, 2:])
    near = jnp.maximum(near, padded[:, 1:-1, :-2])
    valid = 1.0 - near
    count = lax.axis_size("pix") * rows * cols
    values = stack.astype(jnp.float32)
    median = jnp.zeros((bands, rows, cols), jnp.float32)
    for step in range(ITERS + 1):
        numer, denom = local_sums(values, valid, median, step == 0)
        numer, denom = in_one((numer, denom), (("date_0", "date_1"), "date_2"))
        median = (numer + median) / (denom + 1.0)
    first_sum, second_sum = moments(median)
    first_sum, second_sum = packed_total((first_sum, second_sum), "pix")
    return standardize(median, first_sum, second_sum, count)


def solution(mesh):
    torus = Mesh(
        mesh.devices.reshape(8, 4, 2, mesh.shape["pix"]), ("date_0", "date_1", "date_2", "pix")
    )
    placed = (P(DATE, None, "pix", None), P(DATE, "pix", None))
    return jax.shard_map(
        body, mesh=torus, in_specs=placed, out_specs=P(None, "pix", None), check_vma=False
    )
```

profile of v0, /device:TPU:1, one launch (start us, length us, event | category | flops | bytes accessed | tf_op | source)
XLA Modules:
  0.0 175.5 jit_solution(3797479134396852516)
XLA Ops:
  0.0 0.8 subtract_convert_fusion
  0.9 4.0 %collective-permute-start = (bf16[1,1,2048]{2,1,0:T(2,128)(2,1)S(1)}, bf16[1,1,2048]{2,1,0:T(2,128)(2,1)S(1)}, u32[]{:S(2)}, u32[]{:S(2)}) collective-permute-start(bf16[1,1,2048]{2,1,0:T(2,128)(2,1)S(1)} %get-tuple-element.14), channel_id=1, source_target_pairs={{0,1},{1,2},{2,3},{4,5},{5,6},{6,7},{8,9},{9,10},{10,11},{12,13},{... | collective-permute-start | bytes 12296 | tf_op jit(solution)/shard_map/ppermute | solution.py:23
  4.9 1.3 collective-permute-start.1
  6.2 3.1 %collective-permute-done.1 = bf16[1,1,2048]{2,1,0:T(2,128)(2,1)S(1)} collective-permute-done((bf16[1,1,2048]{2,1,0:T(2,128)(2,1)S(1)}, bf16[1,1,2048]{2,1,0:T(2,128)(2,1)S(1)}, u32[]{:S(2)}, u32[]{:S(2)}) %collective-permute-start.1) | collective-permute-done | bytes 4128 | tf_op jit(solution)/shard_map/ppermute | solution.py:25
  9.6 0.8 copy-done
  11.1 6.0 %all_to_all.81 = f32[2,32,2816]{2,1,0:T(8,128)S(1)} all-to-all(f32[2,32,2816]{2,1,0:T(8,128)S(1)} %copy.21), channel_id=1, replica_groups=mesh['date_0'=8,'date_1'=4,'date_2'=2,'pix'=4] {'date_2'}, dimensions={0} | all-to-all | bytes 1441792 | tf_op jit(solution)/shard_map/all_to_all | solution.py:66
  17.4 24.2 %all_to_all.82 = f32[32,1,2816]{2,1,0:T(1,128)S(1)} all-to-all(f32[32,1,2816]{2,1,0:T(1,128)S(1)} %all_to_all.53), channel_id=1, replica_groups=mesh['date_0'=8,'date_1'=4,'date_2'=2,'pix'=4] {'date_0','date_1'}, dimensions={0} | all-to-all | bytes 720896 | tf_op jit(solution)/shard_map/all_to_all | solution.py:73
  42.1 17.0 %all_to_all.83 = f32[32,1,2816]{2,1,0:T(1,128)S(1)} all-to-all(f32[32,1,2816]{2,1,0:T(1,128)S(1)} %broadcast_in_dim.24), channel_id=1, replica_groups=mesh['date_0'=8,'date_1'=4,'date_2'=2,'pix'=4] {'date_0','date_1'}, dimensions={0} | all-to-all | bytes 720896 | tf_op jit(solution)/shard_map/all_to_all | solution.py:41
  59.2 7.1 %all_to_all.84 = f32[2,32,2816]{2,1,0:T(8,128)S(1)} all-to-all(f32[2,32,2816]{2,1,0:T(8,128)S(1)} %broadcast_in_dim.26), channel_id=1, replica_groups=mesh['date_0'=8,'date_1'=4,'date_2'=2,'pix'=4] {'date_2'}, dimensions={0} | all-to-all | bytes 1441792 | tf_op jit(solution)/shard_map/all_to_all | solution.py:41
  66.9 0.6 slice.73
  67.5 0.6 slice.75
  69.0 4.3 %all_to_all.85 = f32[2,32,2816]{2,1,0:T(8,128)S(1)} all-to-all(f32[2,32,2816]{2,1,0:T(8,128)S(1)} %copy.24), channel_id=1, replica_groups=mesh['date_0'=8,'date_1'=4,'date_2'=2,'pix'=4] {'date_2'}, dimensions={0} | all-to-all | bytes 1441792 | tf_op jit(solution)/shard_map/all_to_all | solution.py:66
  73.6 17.1 %all_to_all.86 = f32[32,1,2816]{2,1,0:T(1,128)S(1)} all-to-all(f32[32,1,2816]{2,1,0:T(1,128)S(1)} %all_to_all.58), channel_id=1, replica_groups=mesh['date_0'=8,'date_1'=4,'date_2'=2,'pix'=4] {'date_0','date_1'}, dimensions={0} | all-to-all | bytes 720896 | tf_op jit(solution)/shard_map/all_to_all | solution.py:73
  91.2 17.0 %all_to_all.87 = f32[32,1,2816]{2,1,0:T(1,128)S(1)} all-to-all(f32[32,1,2816]{2,1,0:T(1,128)S(1)} %broadcast_in_dim.28), channel_id=1, replica_groups=mesh['date_0'=8,'date_1'=4,'date_2'=2,'pix'=4] {'date_0','date_1'}, dimensions={0} | all-to-all | bytes 720896 | tf_op jit(solution)/shard_map/all_to_all | solution.py:41
  108.3 7.1 %all_to_all.88 = f32[2,32,2816]{2,1,0:T(8,128)S(1)} all-to-all(f32[2,32,2816]{2,1,0:T(8,128)S(1)} %broadcast_in_dim.30), channel_id=1, replica_groups=mesh['date_0'=8,'date_1'=4,'date_2'=2,'pix'=4] {'date_2'}, dimensions={0} | all-to-all | bytes 1441792 | tf_op jit(solution)/shard_map/all_to_all | solution.py:41
  116.0 0.6 slice.79
  116.6 0.6 slice.77
  118.2 4.3 %all_to_all.89 = f32[2,32,2816]{2,1,0:T(8,128)S(1)} all-to-all(f32[2,32,2816]{2,1,0:T(8,128)S(1)} %copy.27), channel_id=1, replica_groups=mesh['date_0'=8,'date_1'=4,'date_2'=2,'pix'=4] {'date_2'}, dimensions={0} | all-to-all | bytes 1441792 | tf_op jit(solution)/shard_map/all_to_all | solution.py:66
  122.8 17.1 %all_to_all.90 = f32[32,1,2816]{2,1,0:T(1,128)S(1)} all-to-all(f32[32,1,2816]{2,1,0:T(1,128)S(1)} %all_to_all.63), channel_id=1, replica_groups=mesh['date_0'=8,'date_1'=4,'date_2'=2,'pix'=4] {'date_0','date_1'}, dimensions={0} | all-to-all | bytes 720896 | tf_op jit(solution)/shard_map/all_to_all | solution.py:73
  140.3 17.0 %all_to_all.91 = f32[32,1,2816]{2,1,0:T(1,128)S(1)} all-to-all(f32[32,1,2816]{2,1,0:T(1,128)S(1)} %broadcast_in_dim.32), channel_id=1, replica_groups=mesh['date_0'=8,'date_1'=4,'date_2'=2,'pix'=4] {'date_0','date_1'}, dimensions={0} | all-to-all | bytes 720896 | tf_op jit(solution)/shard_map/all_to_all | solution.py:41
  157.4 7.1 %all_to_all.92 = f32[2,32,2816]{2,1,0:T(8,128)S(1)} all-to-all(f32[2,32,2816]{2,1,0:T(8,128)S(1)} %broadcast_in_dim.34), channel_id=1, replica_groups=mesh['date_0'=8,'date_1'=4,'date_2'=2,'pix'=4] {'date_2'}, dimensions={0} | all-to-all | bytes 1441792 | tf_op jit(solution)/shard_map/all_to_all | solution.py:41
  165.1 0.6 slice.83
  166.6 7.8 %all_to_all.93 = f32[4,1,20]{2,1,0:T(1,128)S(1)} all-to-all(f32[4,1,20]{2,1,0:T(1,128)S(1)} %broadcast_in_dim.70), channel_id=1, replica_groups=mesh['date_0'=8,'date_1'=4,'date_2'=2,'pix'=4] {'pix'}, dimensions={0} | all-to-all | bytes 640 | tf_op jit(solution)/shard_map/all_to_all | solution.py:41
  174.6 1.0 subtract_divide_fusion
  (58 shorter events, 7.7 us)
Async XLA Ops:
  0.9 5.3 %collective-permute-start = (bf16[1,1,2048]{2,1,0:T(2,128)(2,1)S(1)}, bf16[1,1,2048]{2,1,0:T(2,128)(2,1)S(1)}, u32[]{:S(2)}, u32[]{:S(2)}) collective-permute-start(bf16[1,1,2048]{2,1,0:T(2,128)(2,1)S(1)} %get-tuple-element.14), channel_id=1, source_target_pairs={{0,1},{1,2},{2,3},{4,5},{5,6},{6,7},{8,9},{9,10},{10,11},{12,13},{... | collective-permute-start | bytes 12296 | tf_op jit(solution)/shard_map/ppermute | solution.py:23
  4.9 4.4 %collective-permute-start.1 = (bf16[1,1,2048]{2,1,0:T(2,128)(2,1)S(1)}, bf16[1,1,2048]{2,1,0:T(2,128)(2,1)S(1)}, u32[]{:S(2)}, u32[]{:S(2)}) collective-permute-start(bf16[1,1,2048]{2,1,0:T(2,128)(2,1)S(1)} %get-tuple-element.15), channel_id=1, source_target_pairs={{1,0},{2,1},{3,2},{5,4},{6,5},{7,6},{9,8},{10,9},{11,10},{13,12},{... | collective-permute-start | bytes 12296 | tf_op jit(solution)/shard_map/ppermute | solution.py:25
  9.4 1.0 copy-start
where the time goes:
time: 176 us
  blocking collectives  153 us (87%)
  local copies, waits for them, and re-layouts  9.22 us (5%)
  starting transfers between devices  5.31 us (3%)
  other arithmetic  4.07 us (2%)
  waiting for transfers between devices  3.09 us (2%)
    all_to_all x7, blocking collectives, from_everyone(): lax.all_to_all(jnp.broadcast_to(shard[None], (count, *shard.shape)), axis...  80.3 us
    all_to_all x3, blocking collectives, summed_rows(): return jnp.sum(lax.all_to_all(own, far, 0, 0, tiled=True), axis=0)  58.4 us
    all_to_all x3, blocking collectives, sum_at_owner(): lax.all_to_all(parts, axis, split_axis=0, concat_axis=0, tiled=True)  14.7 us
    ppermute x1, starting transfers between devices, with_halo(): lax.ppermute(tail, axis, [(i, (i + 1) % count) for i in range(ends)])  4.02 us
  transfers between devices with their start and end apart: 2, of which 1 were waited for; matrix products, arithmetic and copies ran while one was open for 0% of the time, Pallas kernels for 0%

commit v1 on v0

v1 whole, which is shorter than its diff:
```python
import functools

import jax
import jax.numpy as jnp
from jax import lax
from jax.experimental import pallas as pl
from jax.experimental.pallas import tpu as pltpu
from jax.sharding import PartitionSpec as P

ITERS = 2
DELTA_SQ = 0.01
EPS = 1e-05
MESH = pl.DeviceIdType.MESH
Z, X, CORE, Y = 8, 4, 2, 4
PEERS = Z * X * CORE
PAIRS = 4
LANES = 128


def kernel(
    pixels, stack_ref, cloud_ref, out_ref,
    send, recv, hsend, hrecv, vsend, vrecv, work, seen, gath, part, ymom, dmom,
    s_stack, r_stack, s_halo, r_halo, s_valid, r_valid,
    s_z, s_x, s_core, r_gath, s_ymom, r_ymom, s_dmom, r_dmom,
):
    bands = stack_ref.shape[0]
    rows, cols = cloud_ref.shape
    me = lax.axis_index("date")
    y = lax.axis_index("pix")
    z = me // (X * CORE)
    x = (me // CORE) % X
    core = me % CORE

    def date_at(zz, xx, cc):
        return (zz * X + xx) * CORE + cc

    def peer(step):
        return (me + step) % PEERS

    barrier = pltpu.get_barrier_semaphore()

    @pl.loop(1, PEERS)
    def _(step):
        pl.semaphore_signal(barrier, inc=1, device_id={"date": peer(step)}, device_id_type=MESH)

    for step in range(1, Y):
        pl.semaphore_signal(barrier, inc=1, device_id={"pix": (y + step) % Y}, device_id_type=MESH)

    @pl.loop(0, Z)
    def _(zz):
        for cc in range(CORE):
            tile = pl.ds(pl.multiple_of((zz * CORE + cc) * LANES, LANES), LANES)
            for k in range(PAIRS):
                send[date_at(zz, k, cc)] = stack_ref[:, 2 * k : 2 * k + 2, tile]

    recv[me] = send[me]
    cloudy = (1 - cloud_ref[...]).astype(jnp.float32)
    hsend[0] = cloudy[0:1]
    hsend[1] = cloudy[rows - 1 : rows]

    pl.semaphore_wait(barrier, PEERS - 1 + Y - 1)

    halos = []
    for side, to in ((0, (y + Y - 1) % Y), (1, (y + 1) % Y)):
        halos.append(
            pltpu.make_async_remote_copy(
                src_ref=hsend.at[side], dst_ref=hrecv.at[side],
                send_sem=s_halo.at[side], recv_sem=r_halo.at[side],
                device_id={"pix": to}, device_id_type=MESH,
            )
        )
    for copy in halos:
        copy.start()

    @pl.loop(1, PEERS)
    def _(step):
        to = peer(step)
        pltpu.make_async_remote_copy(
            src_ref=send.at[to], dst_ref=recv.at[me], send_sem=s_stack, recv_sem=r_stack.at[me],
            device_id={"date": to}, device_id_type=MESH,
        ).start()

    for copy in halos:
        copy.wait()
    above = jnp.where(y > 0, hrecv[1], 0.0)
    below = jnp.where(y < Y - 1, hrecv[0], 0.0)
    row = lax.broadcasted_iota(jnp.int32, (rows, cols), 0)
    col = lax.broadcasted_iota(jnp.int32, (rows, cols), 1)
    near = jnp.maximum(cloudy, jnp.where(row == 0, above, pltpu.roll(cloudy, 1, 0)))
    near = jnp.maximum(near, jnp.where(row == rows - 1, below, pltpu.roll(cloudy, rows - 1, 0)))
    near = jnp.maximum(near, jnp.where(col == 0, 0.0, pltpu.roll(cloudy, 1, 1)))
    near = jnp.maximum(near, jnp.where(col == cols - 1, 0.0, pltpu.roll(cloudy, cols - 1, 1)))
    valid = 1.0 - near
    for c in range(Z * CORE):
        for k in range(PAIRS):
            block = valid[2 * k : 2 * k + 2, c * LANES : (c + 1) * LANES]
            vsend[date_at(c // CORE, k, c % CORE)] = block.astype(jnp.bfloat16)
    vrecv[me] = vsend[me]

    @pl.loop(1, PEERS)
    def _(step):
        to = peer(step)
        pltpu.make_async_remote_copy(
            src_ref=vsend.at[to], dst_ref=vrecv.at[me], send_sem=s_valid, recv_sem=r_valid.at[me],
            device_id={"date": to}, device_id_type=MESH,
        ).start()

    @pl.loop(0, PEERS)
    def _(step):
        date = peer(step)

        @pl.when(step > 0)
        def _():
            pltpu.make_async_copy(recv.at[date], recv.at[date], r_stack.at[date]).wait()

        block = recv[date].astype(jnp.float32)
        for b in range(bands):
            for r in range(2):
                work[r, b, pl.ds(date, 1), :] = block[b, r : r + 1]

    @pl.loop(0, PEERS)
    def _(step):
        date = peer(step)

        @pl.when(step > 0)
        def _():
            pltpu.make_async_copy(vrecv.at[date], vrecv.at[date], r_valid.at[date]).wait()

        block = vrecv[date].astype(jnp.float32)
        for r in range(2):
            seen[r, pl.ds(date, 1), :] = block[r : r + 1]

    @pl.loop(0, 2)
    def _(r):
        median = [jnp.zeros((1, LANES), jnp.float32)] * bands
        for step in range(ITERS + 1):
            numer = [jnp.zeros((8, LANES), jnp.float32)] * bands
            denom = jnp.zeros((8, LANES), jnp.float32)
            for j in range(0, PEERS, 8):
                values = [work[r, b, j : j + 8, :] for b in range(bands)]
                weight = seen[r, j : j + 8, :]
                if step > 0:
                    square = DELTA_SQ
                    for b in range(bands):
                        diff = values[b] - median[b]
                        square = square + diff * diff
                    weight = weight * lax.rsqrt(square)
                denom = denom + weight
                numer = [n + weight * v for n, v in zip(numer, values)]
            scale = 1.0 / (jnp.sum(denom, axis=0, keepdims=True) + 1.0)
            median = [
                (jnp.sum(n, axis=0, keepdims=True) + m) * scale for n, m in zip(numer, median)
            ]
        for b in range(bands):
            gath[core, x, z, b, pl.ds(r, 1), :] = median[b]
            part[r, b : b + 1, :] = median[b]
            part[r, bands + b : bands + b + 1, :] = median[b] * median[b]

    def pass_on(chunk, send_sem, to):
        pltpu.make_async_remote_copy(
            src_ref=gath.at[chunk], dst_ref=gath.at[chunk],
            send_sem=send_sem, recv_sem=r_gath.at[chunk],
            device_id={"date": to}, device_id_type=MESH,
        ).start()

    def arrived(chunk):
        pltpu.make_async_copy(gath.at[chunk], gath.at[chunk], r_gath.at[chunk]).wait()

    for step in (1, 7, 2, 6, 3, 5, 4):
        pass_on((core, x, z), s_z, date_at((z + step) % Z, x, core))
    for step in (1, 3, 2):
        pass_on((core, x, z), s_x, date_at(z, (x + step) % X, core))
    pass_on((core, x, z), s_core, date_at(z, x, 1 - core))

    sums = jnp.sum(part[0] + part[1], axis=1, keepdims=True)
    lane = lax.broadcasted_iota(jnp.int32, (2 * bands, LANES), 1)
    which = lax.broadcasted_iota(jnp.int32, (2 * bands, LANES), 0)
    ymom[y] = jnp.sum(jnp.where(lane == which, sums, 0.0), axis=0, keepdims=True)
    for step in range(1, Y):
        pltpu.make_async_remote_copy(
            src_ref=ymom.at[y], dst_ref=ymom.at[y], send_sem=s_ymom, recv_sem=r_ymom.at[y],
            device_id={"pix": (y + step) % Y}, device_id_type=MESH,
        ).start()
    for step in range(1, Y):
        other = (y + step) % Y
        pltpu.make_async_copy(ymom.at[other], ymom.at[other], r_ymom.at[other]).wait()
    dmom[me] = (ymom[0] + ymom[1]) + (ymom[2] + ymom[3])

    @pl.loop(1, PEERS)
    def _(step):
        to = peer(step)
        pltpu.make_async_remote_copy(
            src_ref=dmom.at[me], dst_ref=dmom.at[me], send_sem=s_dmom, recv_sem=r_dmom.at[me],
            device_id={"date": to}, device_id_type=MESH,
        ).start()

    for step in (1, 7, 2, 6, 3, 5, 4):
        chunk = (core, x, (z + step) % Z)
        arrived(chunk)
        for hop in (1, 3, 2):
            pass_on(chunk, s_x, date_at(z, (x + hop) % X, core))
        pass_on(chunk, s_core, date_at(z, x, 1 - core))
    for step in (0, 1, 7, 2, 6, 3, 5, 4):
        for hop in (1, 3, 2):
            chunk = (core, (x + hop) % X, (z + step) % Z)
            arrived(chunk)
            pass_on(chunk, s_core, date_at(z, x, 1 - core))

    @pl.loop(1, PEERS)
    def _(step):
        date = peer(step)
        pltpu.make_async_copy(dmom.at[date], dmom.at[date], r_dmom.at[date]).wait()

    total = dmom[0]
    for d in range(1, PEERS):
        total = total + dmom[d]
    lane = lax.broadcasted_iota(jnp.int32, (1, LANES), 1)
    means, scales = [], []
    for b in range(bands):
        mean = jnp.sum(jnp.where(lane == b, total, 0.0), axis=1, keepdims=True) / pixels
        second = jnp.sum(jnp.where(lane == bands + b, total, 0.0), axis=1, keepdims=True) / pixels
        var = second - mean * mean
        means.append(mean)
        scales.append(1.0 / jnp.sqrt(var + EPS))

    @pl.loop(0, X)
    def _(xx):
        @pl.loop(0, Z)
        def _(zz):
            arrived((1 - core, xx, zz))

    @pl.loop(0, Z)
    def _(zz):
        for cc in range(CORE):
            tile = pl.ds(pl.multiple_of((zz * CORE + cc) * LANES, LANES), LANES)
            for b in range(bands):
                block = jnp.concatenate([gath[cc, k, zz, b] for k in range(PAIRS)], axis=0)
                out_ref[b, :, tile] = (block - means[b]) * scales[b]

    pltpu.make_async_copy(send.at[pl.ds(0, PEERS - 1)], send.at[pl.ds(0, PEERS - 1)], s_stack).wait()
    pltpu.make_async_copy(vsend.at[pl.ds(0, PEERS - 1)], vsend.at[pl.ds(0, PEERS - 1)], s_valid).wait()
    pltpu.make_async_copy(dmom.at[pl.ds(0, PEERS - 1)], dmom.at[pl.ds(0, PEERS - 1)], s_dmom).wait()
    pltpu.make_async_copy(ymom.at[pl.ds(0, Y - 1)], ymom.at[pl.ds(0, Y - 1)], s_ymom).wait()
    z_sent = gath.at[0, 0, pl.ds(0, Z - 1)]
    pltpu.make_async_copy(z_sent, z_sent, s_z).wait()
    x_sent = gath.at[0, pl.ds(0, X - 1)]
    pltpu.make_async_copy(x_sent, x_sent, s_x).wait()
    pltpu.make_async_copy(gath.at[0], gath.at[0], s_core).wait()


def body(stack, cloud):
    _, bands, rows, cols = stack.shape
    pixels = float(lax.axis_size("pix") * rows * cols)
    f32, bf16 = jnp.float32, jnp.bfloat16
    dma = pltpu.SemaphoreType.DMA
    return pl.pallas_call(
        functools.partial(kernel, pixels),
        out_shape=jax.ShapeDtypeStruct((bands, rows, cols), f32),
        in_specs=[pl.BlockSpec(memory_space=pltpu.VMEM)] * 2,
        out_specs=pl.BlockSpec(memory_space=pltpu.VMEM),
        scratch_shapes=[
            pltpu.VMEM((PEERS, bands, 2, LANES), bf16),
            pltpu.VMEM((PEERS, bands, 2, LANES), bf16),
            pltpu.VMEM((2, 1, cols), f32),
            pltpu.VMEM((2, 1, cols), f32),
            pltpu.VMEM((PEERS, 2, LANES), bf16),
            pltpu.VMEM((PEERS, 2, LANES), bf16),
            pltpu.VMEM((2, bands, PEERS, LANES), f32),
            pltpu.VMEM((2, PEERS, LANES), f32),
            pltpu.VMEM((CORE, X, Z, bands, 2, LANES), f32),
            pltpu.VMEM((2, 2 * bands, LANES), f32),
            pltpu.VMEM((Y, 1, LANES), f32),
            pltpu.VMEM((PEERS, 1, LANES), f32),
            dma, dma((PEERS,)), dma((2,)), dma((2,)), dma, dma((PEERS,)),
            dma, dma, dma, dma((CORE, X, Z)), dma, dma((Y,)), dma, dma((PEERS,)),
        ],
        compiler_params=pltpu.CompilerParams(collective_id=0, has_side_effects=True),
    )(stack[0], cloud[0])


def solution(mesh):
    placed = (P("date", None, "pix", None), P("date", "pix", None))
    return jax.shard_map(
        body, mesh=mesh, in_specs=placed, out_specs=P(None, "pix", None), check_vma=False
    )
```

time: 176 us -> 42.6 us (0.24)
  blocking collectives: 153 us -> 0 us
  Pallas kernels: 0 us -> 40.5 us
  local copies, waits for them, and re-layouts: 9.22 us -> 1.97 us
  starting transfers between devices: 5.31 us -> 0 us
  other arithmetic: 4.07 us -> 0 us
  waiting for transfers between devices: 3.09 us -> 0 us
    all_to_all x13 -> x0, blocking collectives: 153 us -> none  [the longest x7 80.3 us: from_everyone(): lax.all_to_all(jnp.broadcast_to(shard[None], (count, *shard.shape)), axis...]
    pallas_call x0 -> x1, Pallas kernels: none -> 40.5 us  [body(): pl.pallas_call(functools.partial(kernel, pixels), out_shape=jax.ShapeDtyp...]
    ppermute x2 -> x0, starting transfers between devices: 5.31 us -> none  [the longest x1 4.02 us: with_halo(): lax.ppermute(tail, axis, [(i, (i + 1) % count) for i in range(ends)])]
    slice x7 -> x0, local copies, waits for them, and re-layouts: 3.48 us -> none  [the longest x6 3.47 us: in_one(): total[b:e].reshape(a.shape)]
    ppermute x2 -> x0, waiting for transfers between devices: 3.09 us -> none  [the longest x1 3.08 us: with_halo(): lax.ppermute(head, axis, [((i + 1) % count, i) for i in range(ends)])]
    transpose x6 -> x0, local copies, waits for them, and re-layouts: 1.82 us -> none  [the longest x3 1.67 us: gathered_by_axis(): parts = jnp.swapaxes(from_everyone(first, near), 0, 1)]
  transfers between devices with their start and end apart: 2 -> 0, of which waited for: 1 -> 0; matrix products, arithmetic and copies ran while one was open for 0% -> 0% of each run, Pallas kernels for 0% -> 0%
where the time goes in v1:
time: 42.6 us; the launch traced here: 42.4 us
  Pallas kernels  40.5 us (95%)
  local copies, waits for them, and re-layouts  1.97 us (5%)
    pallas_call x1, Pallas kernels, body(): pl.pallas_call(functools.partial(kernel, pixels), out_shape=jax.ShapeDtyp...  40.5 us
    unnamed x1, local copies, waits for them, and re-layouts  1.97 us

profile of v1, /device:TPU:1, one launch (start us, length us, event | category | flops | bytes accessed | tf_op | source)
XLA Modules:
  0.0 42.4 jit_solution(6551428116763155442)
XLA Ops:
  0.0 40.5 %shard_map.28 = f32[10,8,2048]{2,1,0:T(8,128)} custom-call(bf16[10,8,2048]{2,1,0:T(8,128)(2,1)} %bitcast.2, s32[8,2048]{1,0:T(8,128)} %bitcast.3), custom_call_target="tpu_custom_call" | custom-call | tf_op jit(solution)/shard_map/pallas_call | solution.py:256
  40.5 2.0 %copy.4 = f32[10,8,2048]{2,1,0:T(8,128)} copy(f32[10,8,2048]{2,1,0:T(8,128)} %shard_map.28) | data formatting | bytes 1310720

commit v2 on v1

--- a/solution.py
+++ b/solution.py
@@ -12,16 +12,18 @@
 EPS = 1e-05
 MESH = pl.DeviceIdType.MESH
 Z, X, CORE, Y = 8, 4, 2, 4
-PEERS = Z * X * CORE
+LINE = X * CORE
+PEERS = Z * LINE
 PAIRS = 4
 LANES = 128
 
 
 def kernel(
-    pixels, stack_ref, cloud_ref, out_ref,
-    send, recv, hsend, hrecv, vsend, vrecv, work, seen, gath, part, ymom, dmom,
+    pixels, stack_hbm, cloud_hbm, out_ref,
+    stack_ref, cloud_ref, send, recv, hsend, hrecv, vsend, vrecv, work, seen, gath, part, ymom, dmom,
     s_stack, r_stack, s_halo, r_halo, s_valid, r_valid,
-    s_z, s_x, s_core, r_gath, s_ymom, r_ymom, s_dmom, r_dmom,
+    s_z, s_x, s_core, r_z, r_x, r_core, s_ymom, r_ymom, s_dmom, r_dmom,
+    s_in,
 ):
     bands = stack_ref.shape[0]
     rows, cols = cloud_ref.shape
@@ -37,7 +39,27 @@
     def peer(step):
         return (me + step) % PEERS
 
+    def in_line(zz, step):
+        return zz * LINE + (me % LINE + step) % LINE
+
+    def give(zz, first):
+        @pl.loop(first, LINE)
+        def _(step):
+            to = in_line(zz, step)
+            pltpu.make_async_remote_copy(
+                src_ref=send.at[to], dst_ref=recv.at[me],
+                send_sem=s_stack, recv_sem=r_stack.at[z],
+                device_id={"date": to}, device_id_type=MESH,
+            ).start()
+
+    fetches = [
+        pltpu.make_async_copy(cloud_hbm, cloud_ref, s_in.at[0]),
+        pltpu.make_async_copy(stack_hbm, stack_ref, s_in.at[1]),
+    ]
+
     barrier = pltpu.get_barrier_semaphore()
+    for copy in fetches:
+        copy.start()
 
     @pl.loop(1, PEERS)
     def _(step):
@@ -45,6 +67,9 @@
 
     for step in range(1, Y):
         pl.semaphore_signal(barrier, inc=1, device_id={"pix": (y + step) % Y}, device_id_type=MESH)
+
+    for copy in fetches:
+        copy.wait()
 
     @pl.loop(0, Z)
     def _(zz):
@@ -72,13 +97,9 @@
     for copy in halos:
         copy.start()
 
-    @pl.loop(1, PEERS)
-    def _(step):
-        to = peer(step)
-        pltpu.make_async_remote_copy(
-            src_ref=send.at[to], dst_ref=recv.at[me], send_sem=s_stack, recv_sem=r_stack.at[me],
-            device_id={"date": to}, device_id_type=MESH,
-        ).start()
+    for dz in (4, 3, 5, 2, 6, 1, 7):
+        give((z + dz) % Z, 0)
+    give(z, 1)
 
     for copy in halos:
         copy.wait()
@@ -101,31 +122,36 @@
     def _(step):
         to = peer(step)
         pltpu.make_async_remote_copy(
-            src_ref=vsend.at[to], dst_ref=vrecv.at[me], send_sem=s_valid, recv_sem=r_valid.at[me],
+            src_ref=vsend.at[to], dst_ref=vrecv.at[me], send_sem=s_valid, recv_sem=r_valid,
             device_id={"date": to}, device_id_type=MESH,
         ).start()
 
+    def taken(ref, count, sem):
+        some = ref.at[pl.ds(0, count)]
+        pltpu.make_async_copy(some, some, sem).wait()
+
+    def unpack(zz):
+        @pl.loop(0, LINE)
+        def _(step):
+            date = zz * LINE + step
+            block = recv[date].astype(jnp.float32)
+            for b in range(bands):
+                for r in range(2):
+                    work[r, b, pl.ds(date, 1), :] = block[b, r : r + 1]
+
+    taken(recv, LINE - 1, r_stack.at[z])
+    unpack(z)
+
+    @pl.loop(1, Z)
+    def _(step):
+        zz = (z + step) % Z
+        taken(recv, LINE, r_stack.at[zz])
+        unpack(zz)
+
+    taken(vrecv, PEERS - 1, r_valid)
+
     @pl.loop(0, PEERS)
-    def _(step):
-        date = peer(step)
-
-        @pl.when(step > 0)
-        def _():
-            pltpu.make_async_copy(recv.at[date], recv.at[date], r_stack.at[date]).wait()
-
-        block = recv[date].astype(jnp.float32)
-        for b in range(bands):
-            for r in range(2):
-                work[r, b, pl.ds(date, 1), :] = block[b, r : r + 1]
-
-    @pl.loop(0, PEERS)
-    def _(step):
-        date = peer(step)
-
-        @pl.when(step > 0)
-        def _():
-            pltpu.make_async_copy(vrecv.at[date], vrecv.at[date], r_valid.at[date]).wait()
-
+    def _(date):
         block = vrecv[date].astype(jnp.float32)
         for r in range(2):
             seen[r, pl.ds(date, 1), :] = block[r : r + 1]
@@ -156,21 +182,18 @@
             part[r, b : b + 1, :] = median[b]
             part[r, bands + b : bands + b + 1, :] = median[b] * median[b]
 
-    def pass_on(chunk, send_sem, to):
+    def pass_on(chunk, send_sem, recv_sem, to):
         pltpu.make_async_remote_copy(
             src_ref=gath.at[chunk], dst_ref=gath.at[chunk],
-            send_sem=send_sem, recv_sem=r_gath.at[chunk],
+            send_sem=send_sem, recv_sem=recv_sem,
             device_id={"date": to}, device_id_type=MESH,
         ).start()
 
-    def arrived(chunk):
-        pltpu.make_async_copy(gath.at[chunk], gath.at[chunk], r_gath.at[chunk]).wait()
-
     for step in (1, 7, 2, 6, 3, 5, 4):
-        pass_on((core, x, z), s_z, date_at((z + step) % Z, x, core))
+        pass_on((core, x, z), s_z, r_z.at[z], date_at((z + step) % Z, x, core))
     for step in (1, 3, 2):
-        pass_on((core, x, z), s_x, date_at(z, (x + step) % X, core))
-    pass_on((core, x, z), s_core, date_at(z, x, 1 - core))
+        pass_on((core, x, z), s_x, r_x.at[z], date_at(z, (x + step) % X, core))
+    pass_on((core, x, z), s_core, r_core, date_at(z, x, 1 - core))
 
     sums = jnp.sum(part[0] + part[1], axis=1, keepdims=True)
     lane = lax.broadcasted_iota(jnp.int32, (2 * bands, LANES), 1)
@@ -178,39 +201,39 @@
     ymom[y] = jnp.sum(jnp.where(lane == which, sums, 0.0), axis=0, keepdims=True)
     for step in range(1, Y):
         pltpu.make_async_remote_copy(
-            src_ref=ymom.at[y], dst_ref=ymom.at[y], send_sem=s_ymom, recv_sem=r_ymom.at[y],
+            src_ref=ymom.at[y], dst_ref=ymom.at[y], send_sem=s_ymom, recv_sem=r_ymom,
             device_id={"pix": (y + step) % Y}, device_id_type=MESH,
         ).start()
-    for step in range(1, Y):
-        other = (y + step) % Y
-        pltpu.make_async_copy(ymom.at[other], ymom.at[other], r_ymom.at[other]).wait()
+    def spread(step):
+        zz = (z + step) % Z
+        taken(gath.at[core, x], 1, r_z.at[zz])
+        chunk = (core, x, zz)
+        for hop in (1, 3, 2):
+            pass_on(chunk, s_x, r_x.at[zz], date_at(z, (x + hop) % X, core))
+        pass_on(chunk, s_core, r_core, date_at(z, x, 1 - core))
+
+    spread(1)
+    spread(7)
+    taken(ymom, Y - 1, r_ymom)
     dmom[me] = (ymom[0] + ymom[1]) + (ymom[2] + ymom[3])
 
     @pl.loop(1, PEERS)
     def _(step):
         to = peer(step)
         pltpu.make_async_remote_copy(
-            src_ref=dmom.at[me], dst_ref=dmom.at[me], send_sem=s_dmom, recv_sem=r_dmom.at[me],
+            src_ref=dmom.at[me], dst_ref=dmom.at[me], send_sem=s_dmom, recv_sem=r_dmom,
             device_id={"date": to}, device_id_type=MESH,
         ).start()
 
-    for step in (1, 7, 2, 6, 3, 5, 4):
-        chunk = (core, x, (z + step) % Z)
-        arrived(chunk)
+    for step in (2, 6, 3, 5, 4):
+        spread(step)
+    for step in (0, 1, 7, 2, 6, 3, 5, 4):
+        zz = (z + step) % Z
+        taken(gath.at[core, x], X - 1, r_x.at[zz])
         for hop in (1, 3, 2):
-            pass_on(chunk, s_x, date_at(z, (x + hop) % X, core))
-        pass_on(chunk, s_core, date_at(z, x, 1 - core))
-    for step in (0, 1, 7, 2, 6, 3, 5, 4):
-        for hop in (1, 3, 2):
-            chunk = (core, (x + hop) % X, (z + step) % Z)
-            arrived(chunk)
-            pass_on(chunk, s_core, date_at(z, x, 1 - core))
-
-    @pl.loop(1, PEERS)
-    def _(step):
-        date = peer(step)
-        pltpu.make_async_copy(dmom.at[date], dmom.at[date], r_dmom.at[date]).wait()
-
+            pass_on((core, (x + hop) % X, zz), s_core, r_core, date_at(z, x, 1 - core))
+
+    taken(dmom, PEERS - 1, r_dmom)
     total = dmom[0]
     for d in range(1, PEERS):
         total = total + dmom[d]
@@ -223,11 +246,7 @@
         means.append(mean)
         scales.append(1.0 / jnp.sqrt(var + EPS))
 
-    @pl.loop(0, X)
-    def _(xx):
-        @pl.loop(0, Z)
-        def _(zz):
-            arrived((1 - core, xx, zz))
+    pltpu.make_async_copy(gath.at[0], gath.at[0], r_core).wait()
 
     @pl.loop(0, Z)
     def _(zz):
@@ -237,14 +256,12 @@
                 block = jnp.concatenate([gath[cc, k, zz, b] for k in range(PAIRS)], axis=0)
                 out_ref[b, :, tile] = (block - means[b]) * scales[b]
 
-    pltpu.make_async_copy(send.at[pl.ds(0, PEERS - 1)], send.at[pl.ds(0, PEERS - 1)], s_stack).wait()
-    pltpu.make_async_copy(vsend.at[pl.ds(0, PEERS - 1)], vsend.at[pl.ds(0, PEERS - 1)], s_valid).wait()
-    pltpu.make_async_copy(dmom.at[pl.ds(0, PEERS - 1)], dmom.at[pl.ds(0, PEERS - 1)], s_dmom).wait()
-    pltpu.make_async_copy(ymom.at[pl.ds(0, Y - 1)], ymom.at[pl.ds(0, Y - 1)], s_ymom).wait()
-    z_sent = gath.at[0, 0, pl.ds(0, Z - 1)]
-    pltpu.make_async_copy(z_sent, z_sent, s_z).wait()
-    x_sent = gath.at[0, pl.ds(0, X - 1)]
-    pltpu.make_async_copy(x_sent, x_sent, s_x).wait()
+    taken(send, PEERS - 1, s_stack)
+    taken(vsend, PEERS - 1, s_valid)
+    taken(dmom, PEERS - 1, s_dmom)
+    taken(ymom, Y - 1, s_ymom)
+    taken(gath.at[0, 0], Z - 1, s_z)
+    taken(gath.at[0], X - 1, s_x)
     pltpu.make_async_copy(gath.at[0], gath.at[0], s_core).wait()
 
 
@@ -256,9 +273,11 @@
     return pl.pallas_call(
         functools.partial(kernel, pixels),
         out_shape=jax.ShapeDtypeStruct((bands, rows, cols), f32),
-        in_specs=[pl.BlockSpec(memory_space=pltpu.VMEM)] * 2,
+        in_specs=[pl.BlockSpec(memory_space=pltpu.HBM)] * 2,
         out_specs=pl.BlockSpec(memory_space=pltpu.VMEM),
         scratch_shapes=[
+            pltpu.VMEM((bands, rows, cols), bf16),
+            pltpu.VMEM((rows, cols), jnp.int32),
             pltpu.VMEM((PEERS, bands, 2, LANES), bf16),
             pltpu.VMEM((PEERS, bands, 2, LANES), bf16),
             pltpu.VMEM((2, 1, cols), f32),
@@ -271,11 +290,12 @@
             pltpu.VMEM((2, 2 * bands, LANES), f32),
             pltpu.VMEM((Y, 1, LANES), f32),
             pltpu.VMEM((PEERS, 1, LANES), f32),
-            dma, dma((PEERS,)), dma((2,)), dma((2,)), dma, dma((PEERS,)),
-            dma, dma, dma, dma((CORE, X, Z)), dma, dma((Y,)), dma, dma((PEERS,)),
+            dma, dma((Z,)), dma((2,)), dma((2,)), dma, dma,
+            dma, dma, dma, dma((Z,)), dma((Z,)), dma, dma, dma, dma, dma,
+            dma((2,)),
         ],
-        compiler_params=pltpu.CompilerParams(collective_id=0, has_side_effects=True),
-    )(stack[0], cloud[0])
+        compiler_params=pltpu.CompilerParams(collective_id=0, has_side_effects=True, vmem_limit_bytes=8 << 20),
+    )(pltpu.with_memory_space_constraint(stack[0], pltpu.HBM), pltpu.with_memory_space_constraint(cloud[0], pltpu.HBM))
 
 
 def solution(mesh):

time: 42.6 us -> 36.8 us (0.86)
  Pallas kernels: 40.5 us -> 35.9 us
  local copies, waits for them, and re-layouts: 1.97 us -> 0.84 us
    pallas_call x1, Pallas kernels: 40.5 us -> 35.9 us  [body(): pl.pallas_call(functools.partial(kernel, pixels), out_shape=jax.ShapeDtyp...]
    unnamed x1, local copies, waits for them, and re-layouts: 1.97 us -> 0.84 us
where the time goes in v2:
time: 36.8 us; the launch traced here: 36.7 us
  Pallas kernels  35.9 us (98%)
  local copies, waits for them, and re-layouts  0.84 us (2%)
    pallas_call x1, Pallas kernels, body(): pl.pallas_call(functools.partial(kernel, pixels), out_shape=jax.ShapeDtyp...  35.9 us
    unnamed x1, local copies, waits for them, and re-layouts  0.84 us

profile of v2, /device:TPU:1, one launch (start us, length us, event | category | flops | bytes accessed | tf_op | source)
XLA Modules:
  0.0 36.7 jit_solution(4015128621096347984)
XLA Ops:
  0.0 35.9 %shard_map.28 = f32[10,8,2048]{2,1,0:T(8,128)S(1)} custom-call(bf16[10,8,2048]{2,1,0:T(8,128)(2,1)} %bitcast.2, s32[8,2048]{1,0:T(8,128)} %bitcast.3), custom_call_target="tpu_custom_call" | custom-call | tf_op jit(solution)/shard_map/pallas_call | solution.py:273
  35.9 0.8 %copy.4 = f32[10,8,2048]{2,1,0:T(8,128)} copy(f32[10,8,2048]{2,1,0:T(8,128)S(1)} %shard_map.28) | data formatting | bytes 1310720

commit v3 on v2

--- a/solution.py
+++ b/solution.py
@@ -11,6 +11,9 @@
 DELTA_SQ = 0.01
 EPS = 1e-05
 MESH = pl.DeviceIdType.MESH
+TOP = 32767.0
+MID_COARSE, MID_FINE = 2.0**11, 2.0**26
+POWER = 256.0
 Z, X, CORE, Y = 8, 4, 2, 4
 LINE = X * CORE
 PEERS = Z * LINE
@@ -20,7 +23,7 @@
 
 def kernel(
     pixels, stack_hbm, cloud_hbm, out_ref,
-    stack_ref, cloud_ref, send, recv, hsend, hrecv, vsend, vrecv, work, seen, gath, part, ymom, dmom,
+    stack_ref, cloud_ref, send, recv, hsend, hrecv, vsend, vrecv, work, seen, gath, med, ymom, dmom,
     s_stack, r_stack, s_halo, r_halo, s_valid, r_valid,
     s_z, s_x, s_core, r_z, r_x, r_core, s_ymom, r_ymom, s_dmom, r_dmom,
     s_in,
@@ -178,9 +181,46 @@
                 (jnp.sum(n, axis=0, keepdims=True) + m) * scale for n, m in zip(numer, median)
             ]
         for b in range(bands):
-            gath[core, x, z, b, pl.ds(r, 1), :] = median[b]
-            part[r, b : b + 1, :] = median[b]
-            part[r, bands + b : bands + b + 1, :] = median[b] * median[b]
+            med[r, b : b + 1, :] = median[b]
+
+    first, second = med[0], med[1]
+    lane = lax.broadcasted_iota(jnp.int32, (bands, LANES), 1)
+    band = lax.broadcasted_iota(jnp.int32, (bands, LANES), 0)
+
+    def in_row(*columns):
+        spread_out = jnp.zeros((bands, LANES), jnp.float32)
+        for n, column in enumerate(columns):
+            spread_out = jnp.where(lane == band + n * bands, column, spread_out)
+        return jnp.sum(spread_out, axis=0, keepdims=True)
+
+    ymom[y] = in_row(
+        jnp.sum(first + second, axis=1, keepdims=True),
+        jnp.sum(first * first + second * second, axis=1, keepdims=True),
+    )
+    for step in range(1, Y):
+        pltpu.make_async_remote_copy(
+            src_ref=ymom.at[y], dst_ref=ymom.at[y], send_sem=s_ymom, recv_sem=r_ymom,
+            device_id={"pix": (y + step) % Y}, device_id_type=MESH,
+        ).start()
+
+    high = jnp.max(jnp.maximum(first, second), axis=1, keepdims=True)
+    low = jnp.min(jnp.minimum(first, second), axis=1, keepdims=True)
+    middle = 0.5 * (high + low)
+    coarse = jnp.round(middle * MID_COARSE)
+    fine = jnp.round((middle - coarse / MID_COARSE) * MID_FINE)
+    middle = coarse / MID_COARSE + fine / MID_FINE
+    reach = jnp.maximum(jnp.maximum(high - middle, middle - low), 2.0**-60)
+    power = jnp.ceil(jnp.log2(reach) * POWER) + 1.0
+    to_code = jnp.exp2(power * (-1.0 / POWER)) * TOP
+    codes = [
+        jnp.clip(jnp.round((rows_of - middle) * to_code), -TOP, TOP).astype(jnp.int32)
+        for rows_of in (first, second)
+    ]
+    for b in range(bands):
+        pair = jnp.concatenate([codes[0][b : b + 1], codes[1][b : b + 1]], axis=0)
+        gath[core, x, z, b] = pair.astype(jnp.int16)
+    header = in_row(coarse, fine, power).astype(jnp.int32)
+    gath[core, x, z, bands] = jnp.concatenate([header, header], axis=0).astype(jnp.int16)
 
     def pass_on(chunk, send_sem, recv_sem, to):
         pltpu.make_async_remote_copy(
@@ -193,24 +233,15 @@
         pass_on((core, x, z), s_z, r_z.at[z], date_at((z + step) % Z, x, core))
     for step in (1, 3, 2):
         pass_on((core, x, z), s_x, r_x.at[z], date_at(z, (x + step) % X, core))
-    pass_on((core, x, z), s_core, r_core, date_at(z, x, 1 - core))
-
-    sums = jnp.sum(part[0] + part[1], axis=1, keepdims=True)
-    lane = lax.broadcasted_iota(jnp.int32, (2 * bands, LANES), 1)
-    which = lax.broadcasted_iota(jnp.int32, (2 * bands, LANES), 0)
-    ymom[y] = jnp.sum(jnp.where(lane == which, sums, 0.0), axis=0, keepdims=True)
-    for step in range(1, Y):
-        pltpu.make_async_remote_copy(
-            src_ref=ymom.at[y], dst_ref=ymom.at[y], send_sem=s_ymom, recv_sem=r_ymom,
-            device_id={"pix": (y + step) % Y}, device_id_type=MESH,
-        ).start()
+    pass_on((core, x, z), s_core, r_core.at[z], date_at(z, x, 1 - core))
+
     def spread(step):
         zz = (z + step) % Z
         taken(gath.at[core, x], 1, r_z.at[zz])
         chunk = (core, x, zz)
         for hop in (1, 3, 2):
             pass_on(chunk, s_x, r_x.at[zz], date_at(z, (x + hop) % X, core))
-        pass_on(chunk, s_core, r_core, date_at(z, x, 1 - core))
+        pass_on(chunk, s_core, r_core.at[zz], date_at(z, x, 1 - core))
 
     spread(1)
     spread(7)
@@ -227,34 +258,49 @@
 
     for step in (2, 6, 3, 5, 4):
         spread(step)
+    def tile_of(cc, zz):
+        return pl.ds(pl.multiple_of((zz * CORE + cc) * LANES, LANES), LANES)
+
+    def decode(cc, zz):
+        for b in range(bands):
+            pairs = [gath[cc, k, zz, b].astype(jnp.int32) for k in range(PAIRS)]
+            out_ref[b, :, tile_of(cc, zz)] = jnp.concatenate(pairs, axis=0).astype(jnp.float32)
+
     for step in (0, 1, 7, 2, 6, 3, 5, 4):
         zz = (z + step) % Z
         taken(gath.at[core, x], X - 1, r_x.at[zz])
         for hop in (1, 3, 2):
-            pass_on((core, (x + hop) % X, zz), s_core, r_core, date_at(z, x, 1 - core))
+            pass_on((core, (x + hop) % X, zz), s_core, r_core.at[zz], date_at(z, x, 1 - core))
+        decode(core, zz)
 
     taken(dmom, PEERS - 1, r_dmom)
     total = dmom[0]
     for d in range(1, PEERS):
         total = total + dmom[d]
-    lane = lax.broadcasted_iota(jnp.int32, (1, LANES), 1)
-    means, scales = [], []
-    for b in range(bands):
-        mean = jnp.sum(jnp.where(lane == b, total, 0.0), axis=1, keepdims=True) / pixels
-        second = jnp.sum(jnp.where(lane == bands + b, total, 0.0), axis=1, keepdims=True) / pixels
-        var = second - mean * mean
-        means.append(mean)
-        scales.append(1.0 / jnp.sqrt(var + EPS))
-
-    pltpu.make_async_copy(gath.at[0], gath.at[0], r_core).wait()
-
-    @pl.loop(0, Z)
-    def _(zz):
-        for cc in range(CORE):
-            tile = pl.ds(pl.multiple_of((zz * CORE + cc) * LANES, LANES), LANES)
-            for b in range(bands):
-                block = jnp.concatenate([gath[cc, k, zz, b] for k in range(PAIRS)], axis=0)
-                out_ref[b, :, tile] = (block - means[b]) * scales[b]
+    mean = total / pixels
+    var = pltpu.roll(mean, LANES - bands, 1) - mean * mean
+    scale = 1.0 / jnp.sqrt(var + EPS)
+
+    def finish(cc, zz):
+        ranges = jnp.concatenate(
+            [gath[cc, k, zz, bands].astype(jnp.int32) for k in range(PAIRS)], axis=0
+        ).astype(jnp.float32)
+        fines = pltpu.roll(ranges, LANES - bands, 1)
+        powers = pltpu.roll(ranges, LANES - 2 * bands, 1)
+        middles = ranges / MID_COARSE + fines / MID_FINE
+        gain = jnp.exp2(powers * (1.0 / POWER)) * (1.0 / TOP) * scale
+        shift = (middles - mean) * scale
+        for b in range(bands):
+            block = out_ref[b, :, tile_of(cc, zz)]
+            out_ref[b, :, tile_of(cc, zz)] = block * gain[:, b : b + 1] + shift[:, b : b + 1]
+
+    for step in (0, 1, 7, 2, 6, 3, 5, 4):
+        finish(core, (z + step) % Z)
+    for step in (0, 1, 7, 2, 6, 3, 5, 4):
+        zz = (z + step) % Z
+        taken(gath.at[0, 0], X, r_core.at[zz])
+        decode(1 - core, zz)
+        finish(1 - core, zz)
 
     taken(send, PEERS - 1, s_stack)
     taken(vsend, PEERS - 1, s_valid)
@@ -286,12 +332,12 @@
             pltpu.VMEM((PEERS, 2, LANES), bf16),
             pltpu.VMEM((2, bands, PEERS, LANES), f32),
             pltpu.VMEM((2, PEERS, LANES), f32),
-            pltpu.VMEM((CORE, X, Z, bands, 2, LANES), f32),
-            pltpu.VMEM((2, 2 * bands, LANES), f32),
+            pltpu.VMEM((CORE, X, Z, bands + 1, 2, LANES), jnp.int16),
+            pltpu.VMEM((2, bands, LANES), f32),
             pltpu.VMEM((Y, 1, LANES), f32),
             pltpu.VMEM((PEERS, 1, LANES), f32),
             dma, dma((Z,)), dma((2,)), dma((2,)), dma, dma,
-            dma, dma, dma, dma((Z,)), dma((Z,)), dma, dma, dma, dma, dma,
+            dma, dma, dma, dma((Z,)), dma((Z,)), dma((Z,)), dma, dma, dma, dma,
             dma((2,)),
         ],
         compiler_params=pltpu.CompilerParams(collective_id=0, has_side_effects=True, vmem_limit_bytes=8 << 20),

time: 36.8 us -> 38.5 us (1.046)
  Pallas kernels: 35.9 us -> 37.5 us
    pallas_call x1, Pallas kernels: 35.9 us -> 37.5 us  [body(): pl.pallas_call(functools.partial(kernel, pixels), out_shape=jax.ShapeDtyp...]
where the time goes in v3:
time: 38.5 us; the launch traced here: 38.4 us
  Pallas kernels  37.5 us (97%)
  local copies, waits for them, and re-layouts  0.84 us (2%)
    pallas_call x1, Pallas kernels, body(): pl.pallas_call(functools.partial(kernel, pixels), out_shape=jax.ShapeDtyp...  37.5 us
    unnamed x1, local copies, waits for them, and re-layouts  0.84 us

profile of v3, /device:TPU:1, one launch (start us, length us, event | category | flops | bytes accessed | tf_op | source)
XLA Modules:
  0.0 38.4 jit_solution(6720493518780521562)
XLA Ops:
  0.0 37.5 %shard_map.28 = f32[10,8,2048]{2,1,0:T(8,128)S(1)} custom-call(bf16[10,8,2048]{2,1,0:T(8,128)(2,1)} %bitcast.2, s32[8,2048]{1,0:T(8,128)} %bitcast.3), custom_call_target="tpu_custom_call" | custom-call | tf_op jit(solution)/shard_map/pallas_call | solution.py:319
  37.5 0.8 %copy.4 = f32[10,8,2048]{2,1,0:T(8,128)} copy(f32[10,8,2048]{2,1,0:T(8,128)S(1)} %shard_map.28) | data formatting | bytes 1310720

commit v4 on v2

--- a/solution.py
+++ b/solution.py
@@ -23,7 +23,7 @@
     stack_ref, cloud_ref, send, recv, hsend, hrecv, vsend, vrecv, work, seen, gath, part, ymom, dmom,
     s_stack, r_stack, s_halo, r_halo, s_valid, r_valid,
     s_z, s_x, s_core, r_z, r_x, r_core, s_ymom, r_ymom, s_dmom, r_dmom,
-    s_in,
+    s_in, far,
 ):
     bands = stack_ref.shape[0]
     rows, cols = cloud_ref.shape
@@ -61,9 +61,16 @@
     for copy in fetches:
         copy.start()
 
-    @pl.loop(1, PEERS)
-    def _(step):
-        pl.semaphore_signal(barrier, inc=1, device_id={"date": peer(step)}, device_id_type=MESH)
+    def greet(zz, first):
+        @pl.loop(first, LINE)
+        def _(step):
+            pl.semaphore_signal(
+                barrier, inc=1, device_id={"date": in_line(zz, step)}, device_id_type=MESH
+            )
+
+    for dz in (2, 6, 1, 7):
+        greet((z + dz) % Z, 0)
+    greet(z, 1)
 
     for step in range(1, Y):
         pl.semaphore_signal(barrier, inc=1, device_id={"pix": (y + step) % Y}, device_id_type=MESH)
@@ -83,7 +90,10 @@
     hsend[0] = cloudy[0:1]
     hsend[1] = cloudy[rows - 1 : rows]
 
-    pl.semaphore_wait(barrier, PEERS - 1 + Y - 1)
+    pl.semaphore_wait(barrier, 5 * LINE - 1 + Y - 1)
+    for slot, dz in enumerate((Z - 1, 1, Z - 2)):
+        to = date_at((z + dz) % Z, x, core)
+        pl.semaphore_signal(far.at[slot], inc=1, device_id={"date": to}, device_id_type=MESH)
 
     halos = []
     for side, to in ((0, (y + Y - 1) % Y), (1, (y + 1) % Y)):
@@ -97,9 +107,12 @@
     for copy in halos:
         copy.start()
 
-    for dz in (4, 3, 5, 2, 6, 1, 7):
+    for dz in (2, 6, 1, 7):
         give((z + dz) % Z, 0)
     give(z, 1)
+    for slot, dz in enumerate((3, 5, 4)):
+        pl.semaphore_wait(far.at[slot], 1)
+        give((z + dz) % Z, 0)
 
     for copy in halos:
         copy.wait()
@@ -292,7 +305,7 @@
             pltpu.VMEM((PEERS, 1, LANES), f32),
             dma, dma((Z,)), dma((2,)), dma((2,)), dma, dma,
             dma, dma, dma, dma((Z,)), dma((Z,)), dma, dma, dma, dma, dma,
-            dma((2,)),
+            dma((2,)), pltpu.SemaphoreType.REGULAR((3,)),
         ],
         compiler_params=pltpu.CompilerParams(collective_id=0, has_side_effects=True, vmem_limit_bytes=8 << 20),
     )(pltpu.with_memory_space_constraint(stack[0], pltpu.HBM), pltpu.with_memory_space_constraint(cloud[0], pltpu.HBM))

time: 36.8 us -> 35.2 us (0.957)
  Pallas kernels: 35.9 us -> 34.2 us
    pallas_call x1, Pallas kernels: 35.9 us -> 34.2 us  [body(): pl.pallas_call(functools.partial(kernel, pixels), out_shape=jax.ShapeDtyp...]
where the time goes in v4:
time: 35.2 us; the launch traced here: 35.1 us
  Pallas kernels  34.2 us (97%)
  local copies, waits for them, and re-layouts  0.84 us (2%)
    pallas_call x1, Pallas kernels, body(): pl.pallas_call(functools.partial(kernel, pixels), out_shape=jax.ShapeDtyp...  34.2 us
    unnamed x1, local copies, waits for them, and re-layouts  0.84 us

profile of v4, /device:TPU:1, one launch (start us, length us, event | category | flops | bytes accessed | tf_op | source)
XLA Modules:
  0.0 35.1 jit_solution(409596509731278647)
XLA Ops:
  0.0 34.2 %shard_map.28 = f32[10,8,2048]{2,1,0:T(8,128)S(1)} custom-call(bf16[10,8,2048]{2,1,0:T(8,128)(2,1)} %bitcast.2, s32[8,2048]{1,0:T(8,128)} %bitcast.3), custom_call_target="tpu_custom_call" | custom-call | tf_op jit(solution)/shard_map/pallas_call | solution.py:286
  34.2 0.8 %copy.4 = f32[10,8,2048]{2,1,0:T(8,128)} copy(f32[10,8,2048]{2,1,0:T(8,128)S(1)} %shard_map.28) | data formatting | bytes 1310720

commit v5 on v4

--- a/solution.py
+++ b/solution.py
@@ -144,7 +144,7 @@
         pltpu.make_async_copy(some, some, sem).wait()
 
     def unpack(zz):
-        @pl.loop(0, LINE)
+        @pl.loop(0, LINE, unroll=True)
         def _(step):
             date = zz * LINE + step
             block = recv[date].astype(jnp.float32)
@@ -163,16 +163,16 @@
 
     taken(vrecv, PEERS - 1, r_valid)
 
-    @pl.loop(0, PEERS)
+    @pl.loop(0, PEERS, unroll=8)
     def _(date):
         block = vrecv[date].astype(jnp.float32)
         for r in range(2):
             seen[r, pl.ds(date, 1), :] = block[r : r + 1]
 
-    @pl.loop(0, 2)
-    def _(r):
-        median = [jnp.zeros((1, LANES), jnp.float32)] * bands
-        for step in range(ITERS + 1):
+    medians = [[jnp.zeros((1, LANES), jnp.float32)] * bands for _ in range(2)]
+    for step in range(ITERS + 1):
+        for r in range(2):
+            median = medians[r]
             numer = [jnp.zeros((8, LANES), jnp.float32)] * bands
             denom = jnp.zeros((8, LANES), jnp.float32)
             for j in range(0, PEERS, 8):
@@ -187,13 +187,15 @@
                 denom = denom + weight
                 numer = [n + weight * v for n, v in zip(numer, values)]
             scale = 1.0 / (jnp.sum(denom, axis=0, keepdims=True) + 1.0)
-            median = [
+            medians[r] = [
                 (jnp.sum(n, axis=0, keepdims=True) + m) * scale for n, m in zip(numer, median)
             ]
+    for r in range(2):
         for b in range(bands):
-            gath[core, x, z, b, pl.ds(r, 1), :] = median[b]
-            part[r, b : b + 1, :] = median[b]
-            part[r, bands + b : bands + b + 1, :] = median[b] * median[b]
+            median = medians[r][b]
+            gath[core, x, z, b, r : r + 1, :] = median
+            part[r, b : b + 1, :] = median
+            part[r, bands + b : bands + b + 1, :] = median * median
 
     def pass_on(chunk, send_sem, recv_sem, to):
         pltpu.make_async_remote_copy(
@@ -202,10 +204,20 @@
             device_id={"date": to}, device_id_type=MESH,
         ).start()
 
-    for step in (1, 7, 2, 6, 3, 5, 4):
-        pass_on((core, x, z), s_z, r_z.at[z], date_at((z + step) % Z, x, core))
-    for step in (1, 3, 2):
-        pass_on((core, x, z), s_x, r_x.at[z], date_at(z, (x + step) % X, core))
+    for zz in (0, 1, 7, 2, 6, 3, 5, 4):
+
+        @pl.when(zz != z)
+        def _():
+            pass_on((core, x, z), s_z, r_z.at[z], date_at(zz, x, core))
+
+    def along_x(zz):
+        for xx in (0, 1, 3, 2):
+
+            @pl.when(xx != x)
+            def _():
+                pass_on((core, x, zz), s_x, r_x.at[zz], date_at(z, xx, core))
+
+    along_x(z)
     pass_on((core, x, z), s_core, r_core, date_at(z, x, 1 - core))
 
     sums = jnp.sum(part[0] + part[1], axis=1, keepdims=True)
@@ -221,8 +233,7 @@
         zz = (z + step) % Z
         taken(gath.at[core, x], 1, r_z.at[zz])
         chunk = (core, x, zz)
-        for hop in (1, 3, 2):
-            pass_on(chunk, s_x, r_x.at[zz], date_at(z, (x + hop) % X, core))
+        along_x(zz)
         pass_on(chunk, s_core, r_core, date_at(z, x, 1 - core))
 
     spread(1)
@@ -230,13 +241,14 @@
     taken(ymom, Y - 1, r_ymom)
     dmom[me] = (ymom[0] + ymom[1]) + (ymom[2] + ymom[3])
 
-    @pl.loop(1, PEERS)
-    def _(step):
-        to = peer(step)
-        pltpu.make_async_remote_copy(
-            src_ref=dmom.at[me], dst_ref=dmom.at[me], send_sem=s_dmom, recv_sem=r_dmom,
-            device_id={"date": to}, device_id_type=MESH,
-        ).start()
+    @pl.loop(0, PEERS)
+    def _(to):
+        @pl.when(to != me)
+        def _():
+            pltpu.make_async_remote_copy(
+                src_ref=dmom.at[me], dst_ref=dmom.at[me], send_sem=s_dmom, recv_sem=r_dmom,
+                device_id={"date": to}, device_id_type=MESH,
+            ).start()
 
     for step in (2, 6, 3, 5, 4):
         spread(step)

time: 35.2 us -> 34.6 us (0.983)
  Pallas kernels: 34.2 us -> 33.7 us
    pallas_call x1, Pallas kernels: 34.2 us -> 33.7 us  [body(): pl.pallas_call(functools.partial(kernel, pixels), out_shape=jax.ShapeDtyp...]
where the time goes in v5:
time: 34.6 us
  Pallas kernels  33.7 us (97%)
  local copies, waits for them, and re-layouts  0.84 us (2%)
    pallas_call x1, Pallas kernels, body(): pl.pallas_call(functools.partial(kernel, pixels), out_shape=jax.ShapeDtyp...  33.7 us
    unnamed x1, local copies, waits for them, and re-layouts  0.84 us

profile of v5, /device:TPU:1, one launch (start us, length us, event | category | flops | bytes accessed | tf_op | source)
XLA Modules:
  0.0 34.6 jit_solution(3896842908038980242)
XLA Ops:
  0.0 33.7 %shard_map.28 = f32[10,8,2048]{2,1,0:T(8,128)S(1)} custom-call(bf16[10,8,2048]{2,1,0:T(8,128)(2,1)} %bitcast.2, s32[8,2048]{1,0:T(8,128)} %bitcast.3), custom_call_target="tpu_custom_call" | custom-call | tf_op jit(solution)/shard_map/pallas_call | solution.py:298
  33.7 0.8 %copy.4 = f32[10,8,2048]{2,1,0:T(8,128)} copy(f32[10,8,2048]{2,1,0:T(8,128)S(1)} %shard_map.28) | data formatting | bytes 1310720

commit v6 on v5

--- a/solution.py
+++ b/solution.py
@@ -15,15 +15,16 @@
 LINE = X * CORE
 PEERS = Z * LINE
 PAIRS = 4
+ELDEST = 1
 LANES = 128
 
 
 def kernel(
     pixels, stack_hbm, cloud_hbm, out_ref,
-    stack_ref, cloud_ref, send, recv, hsend, hrecv, vsend, vrecv, work, seen, gath, part, ymom, dmom,
+    stack_ref, cloud_ref, send, recv, hsend, hrecv, vsend, vrecv, work, seen, gath, part, ymom, dmom, every, whole,
     s_stack, r_stack, s_halo, r_halo, s_valid, r_valid,
     s_z, s_x, s_core, r_z, r_x, r_core, s_ymom, r_ymom, s_dmom, r_dmom,
-    s_in, far,
+    s_in, far, s_every, r_every,
 ):
     bands = stack_ref.shape[0]
     rows, cols = cloud_ref.shape
@@ -229,6 +230,17 @@
             src_ref=ymom.at[y], dst_ref=ymom.at[y], send_sem=s_ymom, recv_sem=r_ymom,
             device_id={"pix": (y + step) % Y}, device_id_type=MESH,
         ).start()
+
+    eldest = (me == ELDEST) & (y == 0)
+    others = (me != ELDEST) | (y != 0)
+    every[y * PEERS + me] = ymom[y]
+
+    @pl.when(others)
+    def _():
+        pltpu.make_async_remote_copy(
+            src_ref=every.at[y * PEERS + me], dst_ref=every.at[y * PEERS + me], send_sem=s_every, recv_sem=r_every,
+            device_id={"date": ELDEST, "pix": 0}, device_id_type=MESH,
+        ).start()
     def spread(step):
         zz = (z + step) % Z
         taken(gath.at[core, x], 1, r_z.at[zz])
@@ -243,7 +255,7 @@
 
     @pl.loop(0, PEERS)
     def _(to):
-        @pl.when(to != me)
+        @pl.when((to != me) & ((to != ELDEST) | (y != 0)))
         def _():
             pltpu.make_async_remote_copy(
                 src_ref=dmom.at[me], dst_ref=dmom.at[me], send_sem=s_dmom, recv_sem=r_dmom,
@@ -258,10 +270,27 @@
         for hop in (1, 3, 2):
             pass_on((core, (x + hop) % X, zz), s_core, r_core, date_at(z, x, 1 - core))
 
-    taken(dmom, PEERS - 1, r_dmom)
-    total = dmom[0]
-    for d in range(1, PEERS):
-        total = total + dmom[d]
+    @pl.when(others)
+    def _():
+        taken(dmom, PEERS - 1, r_dmom)
+        total = dmom[0]
+        for d in range(1, PEERS):
+            total = total + dmom[d]
+        whole[...] = total
+
+    @pl.when(eldest)
+    def _():
+        taken(every, Y * PEERS - 1, r_every)
+
+        def of_date(d):
+            return (every[d] + every[PEERS + d]) + (every[2 * PEERS + d] + every[3 * PEERS + d])
+
+        total = of_date(0)
+        for d in range(1, PEERS):
+            total = total + of_date(d)
+        whole[...] = total
+
+    total = whole[...]
     lane = lax.broadcasted_iota(jnp.int32, (1, LANES), 1)
     means, scales = [], []
     for b in range(bands):
@@ -283,7 +312,18 @@
 
     taken(send, PEERS - 1, s_stack)
     taken(vsend, PEERS - 1, s_valid)
-    taken(dmom, PEERS - 1, s_dmom)
+    @pl.when(others & (y == 0))
+    def _():
+        taken(dmom, PEERS - 2, s_dmom)
+
+    @pl.when(eldest | (y != 0))
+    def _():
+        taken(dmom, PEERS - 1, s_dmom)
+
+    @pl.when(others)
+    def _():
+        taken(every, 1, s_every)
+
     taken(ymom, Y - 1, s_ymom)
     taken(gath.at[0, 0], Z - 1, s_z)
     taken(gath.at[0], X - 1, s_x)
@@ -315,9 +355,11 @@
             pltpu.VMEM((2, 2 * bands, LANES), f32),
             pltpu.VMEM((Y, 1, LANES), f32),
             pltpu.VMEM((PEERS, 1, LANES), f32),
+            pltpu.VMEM((Y * PEERS, 1, LANES), f32),
+            pltpu.VMEM((1, LANES), f32),
             dma, dma((Z,)), dma((2,)), dma((2,)), dma, dma,
             dma, dma, dma, dma((Z,)), dma((Z,)), dma, dma, dma, dma, dma,
-            dma((2,)), pltpu.SemaphoreType.REGULAR((3,)),
+            dma((2,)), pltpu.SemaphoreType.REGULAR((3,)), dma, dma,
         ],
         compiler_params=pltpu.CompilerParams(collective_id=0, has_side_effects=True, vmem_limit_bytes=8 << 20),
     )(pltpu.with_memory_space_constraint(stack[0], pltpu.HBM), pltpu.with_memory_space_constraint(cloud[0], pltpu.HBM))

time: 34.6 us -> 34.2 us (0.988)
  Pallas kernels: 33.7 us -> 33.3 us
    pallas_call x1, Pallas kernels: 33.7 us -> 33.3 us  [body(): pl.pallas_call(functools.partial(kernel, pixels), out_shape=jax.ShapeDtyp...]
where the time goes in v6:
time: 34.2 us; the launch traced here: 34.1 us
  Pallas kernels  33.3 us (97%)
  local copies, waits for them, and re-layouts  0.84 us (2%)
    pallas_call x1, Pallas kernels, body(): pl.pallas_call(functools.partial(kernel, pixels), out_shape=jax.ShapeDtyp...  33.3 us
    unnamed x1, local copies, waits for them, and re-layouts  0.84 us

profile of v6, /device:TPU:1, one launch (start us, length us, event | category | flops | bytes accessed | tf_op | source)
XLA Modules:
  0.0 34.1 jit_solution(6232589044008359102)
XLA Ops:
  0.0 33.3 %shard_map.28 = f32[10,8,2048]{2,1,0:T(8,128)S(1)} custom-call(bf16[10,8,2048]{2,1,0:T(8,128)(2,1)} %bitcast.2, s32[8,2048]{1,0:T(8,128)} %bitcast.3), custom_call_target="tpu_custom_call" | custom-call | tf_op jit(solution)/shard_map/pallas_call | solution.py:338
  33.3 0.8 %copy.4 = f32[10,8,2048]{2,1,0:T(8,128)} copy(f32[10,8,2048]{2,1,0:T(8,128)S(1)} %shard_map.28) | data formatting | bytes 1310720

commit v7 on v6

--- a/solution.py
+++ b/solution.py
@@ -24,7 +24,7 @@
     stack_ref, cloud_ref, send, recv, hsend, hrecv, vsend, vrecv, work, seen, gath, part, ymom, dmom, every, whole,
     s_stack, r_stack, s_halo, r_halo, s_valid, r_valid,
     s_z, s_x, s_core, r_z, r_x, r_core, s_ymom, r_ymom, s_dmom, r_dmom,
-    s_in, far, s_every, r_every,
+    s_in, far, s_every, r_every, s_mid, s_late, s_far,
 ):
     bands = stack_ref.shape[0]
     rows, cols = cloud_ref.shape
@@ -108,9 +108,8 @@
     for copy in halos:
         copy.start()
 
-    for dz in (2, 6, 1, 7):
+    for dz in (2, 6):
         give((z + dz) % Z, 0)
-    give(z, 1)
     for slot, dz in enumerate((3, 5, 4)):
         pl.semaphore_wait(far.at[slot], 1)
         give((z + dz) % Z, 0)
@@ -140,63 +139,71 @@
             device_id={"date": to}, device_id_type=MESH,
         ).start()
 
+    for dz in (1, 7):
+        give((z + dz) % Z, 0)
+    give(z, 1)
+
     def taken(ref, count, sem):
         some = ref.at[pl.ds(0, count)]
         pltpu.make_async_copy(some, some, sem).wait()
 
+    def rows_of(zz):
+        return pl.ds(pl.multiple_of(2 * LINE * zz, 2 * LINE), 2 * LINE)
+
     def unpack(zz):
-        @pl.loop(0, LINE, unroll=True)
-        def _(step):
-            date = zz * LINE + step
-            block = recv[date].astype(jnp.float32)
+        for step in range(LINE):
+            block = recv[zz * LINE + step].astype(jnp.float32)
             for b in range(bands):
-                for r in range(2):
-                    work[r, b, pl.ds(date, 1), :] = block[b, r : r + 1]
-
-    taken(recv, LINE - 1, r_stack.at[z])
-    unpack(z)
-
-    @pl.loop(1, Z)
+                work.at[b, rows_of(zz)][2 * step : 2 * step + 2, :] = block[b]
+
+    @pl.loop(2, Z - 1)
     def _(step):
         zz = (z + step) % Z
         taken(recv, LINE, r_stack.at[zz])
         unpack(zz)
 
+    for step in (1, Z - 1):
+        zz = (z + step) % Z
+        taken(recv, LINE, r_stack.at[zz])
+        unpack(zz)
+
+    taken(recv, LINE - 1, r_stack.at[z])
+    unpack(z)
+
     taken(vrecv, PEERS - 1, r_valid)
 
-    @pl.loop(0, PEERS, unroll=8)
-    def _(date):
-        block = vrecv[date].astype(jnp.float32)
-        for r in range(2):
-            seen[r, pl.ds(date, 1), :] = block[r : r + 1]
-
-    medians = [[jnp.zeros((1, LANES), jnp.float32)] * bands for _ in range(2)]
+    @pl.loop(0, Z)
+    def _(zz):
+        for step in range(LINE):
+            block = vrecv[zz * LINE + step].astype(jnp.float32)
+            seen.at[rows_of(zz)][2 * step : 2 * step + 2, :] = block
+
+    def over_dates(sums):
+        sums = sums + pltpu.roll(sums, 2, 0)
+        return sums + pltpu.roll(sums, 4, 0)
+
+    median = [jnp.zeros((8, LANES), jnp.float32)] * bands
     for step in range(ITERS + 1):
-        for r in range(2):
-            median = medians[r]
-            numer = [jnp.zeros((8, LANES), jnp.float32)] * bands
-            denom = jnp.zeros((8, LANES), jnp.float32)
-            for j in range(0, PEERS, 8):
-                values = [work[r, b, j : j + 8, :] for b in range(bands)]
-                weight = seen[r, j : j + 8, :]
-                if step > 0:
-                    square = DELTA_SQ
-                    for b in range(bands):
-                        diff = values[b] - median[b]
-                        square = square + diff * diff
-                    weight = weight * lax.rsqrt(square)
-                denom = denom + weight
-                numer = [n + weight * v for n, v in zip(numer, values)]
-            scale = 1.0 / (jnp.sum(denom, axis=0, keepdims=True) + 1.0)
-            medians[r] = [
-                (jnp.sum(n, axis=0, keepdims=True) + m) * scale for n, m in zip(numer, median)
-            ]
-    for r in range(2):
-        for b in range(bands):
-            median = medians[r][b]
-            gath[core, x, z, b, r : r + 1, :] = median
-            part[r, b : b + 1, :] = median
-            part[r, bands + b : bands + b + 1, :] = median * median
+        numer = [jnp.zeros((8, LANES), jnp.float32)] * bands
+        denom = jnp.zeros((8, LANES), jnp.float32)
+        for j in range(0, 2 * PEERS, 8):
+            values = [work[b, j : j + 8, :] for b in range(bands)]
+            weight = seen[j : j + 8, :]
+            if step > 0:
+                square = DELTA_SQ
+                for b in range(bands):
+                    diff = values[b] - median[b]
+                    square = square + diff * diff
+                weight = weight * lax.rsqrt(square)
+            denom = denom + weight
+            numer = [n + weight * v for n, v in zip(numer, values)]
+        scale = 1.0 / (over_dates(denom) + 1.0)
+        median = [(over_dates(n) + m) * scale for n, m in zip(numer, median)]
+    for b in range(bands):
+        gath[core, x, z, b] = median[b][0:2]
+        square = median[b] * median[b]
+        part[b : b + 1, :] = median[b][0:1] + median[b][1:2]
+        part[bands + b : bands + b + 1, :] = square[0:1] + square[1:2]
 
     def pass_on(chunk, send_sem, recv_sem, to):
         pltpu.make_async_remote_copy(
@@ -218,10 +225,16 @@
             def _():
                 pass_on((core, x, zz), s_x, r_x.at[zz], date_at(z, xx, core))
 
+    distant = (z >= 3) & (z <= 5) & (x != 0) & (core == 0)
+
+    @pl.when(distant)
+    def _():
+        pass_on((core, x, z), s_far, r_core, ELDEST)
+
     along_x(z)
     pass_on((core, x, z), s_core, r_core, date_at(z, x, 1 - core))
 
-    sums = jnp.sum(part[0] + part[1], axis=1, keepdims=True)
+    sums = jnp.sum(part[...], axis=1, keepdims=True)
     lane = lax.broadcasted_iota(jnp.int32, (2 * bands, LANES), 1)
     which = lax.broadcasted_iota(jnp.int32, (2 * bands, LANES), 0)
     ymom[y] = jnp.sum(jnp.where(lane == which, sums, 0.0), axis=0, keepdims=True)
@@ -264,11 +277,23 @@
 
     for step in (2, 6, 3, 5, 4):
         spread(step)
+    elsewhere = (z != 0) | (x != 0) | (core != 0)
     for step in (0, 1, 7, 2, 6, 3, 5, 4):
         zz = (z + step) % Z
         taken(gath.at[core, x], X - 1, r_x.at[zz])
-        for hop in (1, 3, 2):
-            pass_on((core, (x + hop) % X, zz), s_core, r_core, date_at(z, x, 1 - core))
+
+        def hand_over(send_sem):
+            for hop in (1, 3, 2):
+                pass_on((core, (x + hop) % X, zz), send_sem, r_core, date_at(z, x, 1 - core))
+
+        if step in (3, 5, 4):
+
+            @pl.when(elsewhere)
+            def _():
+                hand_over(s_late)
+
+        else:
+            hand_over(s_mid)
 
     @pl.when(others)
     def _():
@@ -327,7 +352,18 @@
     taken(ymom, Y - 1, s_ymom)
     taken(gath.at[0, 0], Z - 1, s_z)
     taken(gath.at[0], X - 1, s_x)
-    pltpu.make_async_copy(gath.at[0], gath.at[0], s_core).wait()
+    taken(gath.at[0], 1, s_core)
+    mid = gath.at[0, pl.ds(0, X - 1), pl.ds(0, Z - 3)]
+    pltpu.make_async_copy(mid, mid, s_mid).wait()
+
+    @pl.when(elsewhere)
+    def _():
+        late = gath.at[0, pl.ds(0, X - 1), pl.ds(0, 3)]
+        pltpu.make_async_copy(late, late, s_late).wait()
+
+    @pl.when(distant)
+    def _():
+        taken(gath.at[0, 0], 1, s_far)
 
 
 def body(stack, cloud):
@@ -349,17 +385,17 @@
             pltpu.VMEM((2, 1, cols), f32),
             pltpu.VMEM((PEERS, 2, LANES), bf16),
             pltpu.VMEM((PEERS, 2, LANES), bf16),
-            pltpu.VMEM((2, bands, PEERS, LANES), f32),
-            pltpu.VMEM((2, PEERS, LANES), f32),
+            pltpu.VMEM((bands, 2 * PEERS, LANES), f32),
+            pltpu.VMEM((2 * PEERS, LANES), f32),
             pltpu.VMEM((CORE, X, Z, bands, 2, LANES), f32),
-            pltpu.VMEM((2, 2 * bands, LANES), f32),
+            pltpu.VMEM((2 * bands, LANES), f32),
             pltpu.VMEM((Y, 1, LANES), f32),
             pltpu.VMEM((PEERS, 1, LANES), f32),
             pltpu.VMEM((Y * PEERS, 1, LANES), f32),
             pltpu.VMEM((1, LANES), f32),
             dma, dma((Z,)), dma((2,)), dma((2,)), dma, dma,
             dma, dma, dma, dma((Z,)), dma((Z,)), dma, dma, dma, dma, dma,
-            dma((2,)), pltpu.SemaphoreType.REGULAR((3,)), dma, dma,
+            dma((2,)), pltpu.SemaphoreType.REGULAR((3,)), dma, dma, dma, dma, dma,
         ],
         compiler_params=pltpu.CompilerParams(collective_id=0, has_side_effects=True, vmem_limit_bytes=8 << 20),
     )(pltpu.with_memory_space_constraint(stack[0], pltpu.HBM), pltpu.with_memory_space_constraint(cloud[0], pltpu.HBM))

time: 34.2 us -> 33.3 us (0.974)
  Pallas kernels: 33.3 us -> 32.3 us
    pallas_call x1, Pallas kernels: 33.3 us -> 32.3 us  [body(): pl.pallas_call(functools.partial(kernel, pixels), out_shape=jax.ShapeDtyp...]
where the time goes in v7:
time: 33.3 us; the launch traced here: 33.2 us
  Pallas kernels  32.3 us (97%)
  local copies, waits for them, and re-layouts  0.84 us (3%)
    pallas_call x1, Pallas kernels, body(): pl.pallas_call(functools.partial(kernel, pixels), out_shape=jax.ShapeDtyp...  32.3 us
    unnamed x1, local copies, waits for them, and re-layouts  0.84 us

profile of v7, /device:TPU:1, one launch (start us, length us, event | category | flops | bytes accessed | tf_op | source)
XLA Modules:
  0.0 33.2 jit_solution(8548342510174900502)
XLA Ops:
  0.0 32.3 %shard_map.28 = f32[10,8,2048]{2,1,0:T(8,128)S(1)} custom-call(bf16[10,8,2048]{2,1,0:T(8,128)(2,1)} %bitcast.2, s32[8,2048]{1,0:T(8,128)} %bitcast.3), custom_call_target="tpu_custom_call" | custom-call | tf_op jit(solution)/shard_map/pallas_call | solution.py:374
  32.3 0.8 %copy.4 = f32[10,8,2048]{2,1,0:T(8,128)} copy(f32[10,8,2048]{2,1,0:T(8,128)S(1)} %shard_map.28) | data formatting | bytes 1310720

commit v8 on v7

--- a/solution.py
+++ b/solution.py
@@ -325,15 +325,17 @@
         means.append(mean)
         scales.append(1.0 / jnp.sqrt(var + EPS))
 
-    pltpu.make_async_copy(gath.at[0], gath.at[0], r_core).wait()
-
-    @pl.loop(0, Z)
-    def _(zz):
-        for cc in range(CORE):
+    def settle(cc):
+        @pl.loop(0, Z)
+        def _(zz):
             tile = pl.ds(pl.multiple_of((zz * CORE + cc) * LANES, LANES), LANES)
             for b in range(bands):
                 block = jnp.concatenate([gath[cc, k, zz, b] for k in range(PAIRS)], axis=0)
                 out_ref[b, :, tile] = (block - means[b]) * scales[b]
+
+    settle(core)
+    pltpu.make_async_copy(gath.at[0], gath.at[0], r_core).wait()
+    settle(1 - core)
 
     taken(send, PEERS - 1, s_stack)
     taken(vsend, PEERS - 1, s_valid)

time: 33.3 us -> 33.2 us (level)
  no operation moved by 1% of the time
where the time goes in v8:
time: 33.2 us; the launch traced here: 33.1 us
  Pallas kernels  32.2 us (97%)
  local copies, waits for them, and re-layouts  0.84 us (3%)
    pallas_call x1, Pallas kernels, body(): pl.pallas_call(functools.partial(kernel, pixels), out_shape=jax.ShapeDtyp...  32.2 us
    unnamed x1, local copies, waits for them, and re-layouts  0.84 us

profile of v8, /device:TPU:1, one launch (start us, length us, event | category | flops | bytes accessed | tf_op | source)
XLA Modules:
  0.0 33.1 jit_solution(18406123296929733869)
XLA Ops:
  0.0 32.2 %shard_map.28 = f32[10,8,2048]{2,1,0:T(8,128)S(1)} custom-call(bf16[10,8,2048]{2,1,0:T(8,128)(2,1)} %bitcast.2, s32[8,2048]{1,0:T(8,128)} %bitcast.3), custom_call_target="tpu_custom_call" | custom-call | tf_op jit(solution)/shard_map/pallas_call | solution.py:376
  32.2 0.8 %copy.4 = f32[10,8,2048]{2,1,0:T(8,128)} copy(f32[10,8,2048]{2,1,0:T(8,128)S(1)} %shard_map.28) | data formatting | bytes 1310720

commit v9 on v7

--- a/solution.py
+++ b/solution.py
@@ -229,10 +229,10 @@
 
     @pl.when(distant)
     def _():
-        pass_on((core, x, z), s_far, r_core, ELDEST)
+        pass_on((core, x, z), s_far, r_core.at[1], ELDEST)
 
     along_x(z)
-    pass_on((core, x, z), s_core, r_core, date_at(z, x, 1 - core))
+    pass_on((core, x, z), s_core, r_core.at[0], date_at(z, x, 1 - core))
 
     sums = jnp.sum(part[...], axis=1, keepdims=True)
     lane = lax.broadcasted_iota(jnp.int32, (2 * bands, LANES), 1)
@@ -259,7 +259,7 @@
         taken(gath.at[core, x], 1, r_z.at[zz])
         chunk = (core, x, zz)
         along_x(zz)
-        pass_on(chunk, s_core, r_core, date_at(z, x, 1 - core))
+        pass_on(chunk, s_core, r_core.at[int(step in (3, 5, 4))], date_at(z, x, 1 - core))
 
     spread(1)
     spread(7)
@@ -284,7 +284,7 @@
 
         def hand_over(send_sem):
             for hop in (1, 3, 2):
-                pass_on((core, (x + hop) % X, zz), send_sem, r_core, date_at(z, x, 1 - core))
+                pass_on((core, (x + hop) % X, zz), send_sem, r_core.at[int(step in (3, 5, 4))], date_at(z, x, 1 - core))
 
         if step in (3, 5, 4):
 
@@ -325,15 +325,20 @@
         means.append(mean)
         scales.append(1.0 / jnp.sqrt(var + EPS))
 
-    pltpu.make_async_copy(gath.at[0], gath.at[0], r_core).wait()
-
-    @pl.loop(0, Z)
-    def _(zz):
-        for cc in range(CORE):
+    def settle(cc, start, count):
+        @pl.loop(0, count)
+        def _(step):
+            zz = (z + start + step) % Z
             tile = pl.ds(pl.multiple_of((zz * CORE + cc) * LANES, LANES), LANES)
             for b in range(bands):
                 block = jnp.concatenate([gath[cc, k, zz, b] for k in range(PAIRS)], axis=0)
                 out_ref[b, :, tile] = (block - means[b]) * scales[b]
+
+    settle(core, 0, Z)
+    for group, start, count in ((0, Z - 2, 5), (1, 3, 3)):
+        part_of = gath.at[0, :, pl.ds(0, count)]
+        pltpu.make_async_copy(part_of, part_of, r_core.at[group]).wait()
+        settle(1 - core, start, count)
 
     taken(send, PEERS - 1, s_stack)
     taken(vsend, PEERS - 1, s_valid)
@@ -394,7 +399,7 @@
             pltpu.VMEM((Y * PEERS, 1, LANES), f32),
             pltpu.VMEM((1, LANES), f32),
             dma, dma((Z,)), dma((2,)), dma((2,)), dma, dma,
-            dma, dma, dma, dma((Z,)), dma((Z,)), dma, dma, dma, dma, dma,
+            dma, dma, dma, dma((Z,)), dma((Z,)), dma((2,)), dma, dma, dma, dma,
             dma((2,)), pltpu.SemaphoreType.REGULAR((3,)), dma, dma, dma, dma, dma,
         ],
         compiler_params=pltpu.CompilerParams(collective_id=0, has_side_effects=True, vmem_limit_bytes=8 << 20),

time: 33.3 us -> 33.2 us (level)
  no operation moved by 1% of the time
where the time goes in v9:
time: 33.2 us; the launch traced here: 33.1 us
  Pallas kernels  32.3 us (97%)
  local copies, waits for them, and re-layouts  0.84 us (3%)
    pallas_call x1, Pallas kernels, body(): pl.pallas_call(functools.partial(kernel, pixels), out_shape=jax.ShapeDtyp...  32.3 us
    unnamed x1, local copies, waits for them, and re-layouts  0.84 us

profile of v9, /device:TPU:1, one launch (start us, length us, event | category | flops | bytes accessed | tf_op | source)
XLA Modules:
  0.0 33.1 jit_solution(1174541480114165492)
XLA Ops:
  0.0 32.3 %shard_map.28 = f32[10,8,2048]{2,1,0:T(8,128)S(1)} custom-call(bf16[10,8,2048]{2,1,0:T(8,128)(2,1)} %bitcast.2, s32[8,2048]{1,0:T(8,128)} %bitcast.3), custom_call_target="tpu_custom_call" | custom-call | tf_op jit(solution)/shard_map/pallas_call | solution.py:379
  32.3 0.8 %copy.4 = f32[10,8,2048]{2,1,0:T(8,128)} copy(f32[10,8,2048]{2,1,0:T(8,128)S(1)} %shard_map.28) | data formatting | bytes 1310720

commit v10 on v8

--- a/solution.py
+++ b/solution.py
@@ -101,7 +101,7 @@
         halos.append(
             pltpu.make_async_remote_copy(
                 src_ref=hsend.at[side], dst_ref=hrecv.at[side],
-                send_sem=s_halo.at[side], recv_sem=r_halo.at[side],
+                send_sem=s_halo, recv_sem=r_halo,
                 device_id={"pix": to}, device_id_type=MESH,
             )
         )
@@ -114,8 +114,8 @@
         pl.semaphore_wait(far.at[slot], 1)
         give((z + dz) % Z, 0)
 
-    for copy in halos:
-        copy.wait()
+    pltpu.make_async_copy(hsend, hsend, s_halo).wait()
+    pltpu.make_async_copy(hrecv, hrecv, r_halo).wait()
     above = jnp.where(y > 0, hrecv[1], 0.0)
     below = jnp.where(y < Y - 1, hrecv[0], 0.0)
     row = lax.broadcasted_iota(jnp.int32, (rows, cols), 0)
@@ -395,7 +395,7 @@
             pltpu.VMEM((PEERS, 1, LANES), f32),
             pltpu.VMEM((Y * PEERS, 1, LANES), f32),
             pltpu.VMEM((1, LANES), f32),
-            dma, dma((Z,)), dma((2,)), dma((2,)), dma, dma,
+            dma, dma((Z,)), dma, dma, dma, dma,
             dma, dma, dma, dma((Z,)), dma((Z,)), dma, dma, dma, dma, dma,
             dma((2,)), pltpu.SemaphoreType.REGULAR((3,)), dma, dma, dma, dma, dma,
         ],

time: 33.2 us -> 33.1 us (level)
  no operation moved by 1% of the time
where the time goes in v10:
time: 33.1 us
  Pallas kernels  32.2 us (97%)
  local copies, waits for them, and re-layouts  0.84 us (3%)
    pallas_call x1, Pallas kernels, body(): pl.pallas_call(functools.partial(kernel, pixels), out_shape=jax.ShapeDtyp...  32.2 us
    unnamed x1, local copies, waits for them, and re-layouts  0.84 us

profile of v10, /device:TPU:1, one launch (start us, length us, event | category | flops | bytes accessed | tf_op | source)
XLA Modules:
  0.0 33.1 jit_solution(5571735817160782202)
XLA Ops:
  0.0 32.2 %shard_map.28 = f32[10,8,2048]{2,1,0:T(8,128)S(1)} custom-call(bf16[10,8,2048]{2,1,0:T(8,128)(2,1)} %bitcast.2, s32[8,2048]{1,0:T(8,128)} %bitcast.3), custom_call_target="tpu_custom_call" | custom-call | tf_op jit(solution)/shard_map/pallas_call | solution.py:376
  32.2 0.8 %copy.4 = f32[10,8,2048]{2,1,0:T(8,128)} copy(f32[10,8,2048]{2,1,0:T(8,128)S(1)} %shard_map.28) | data formatting | bytes 1310720
